TPU v7x, 32 devices: a whole 2x2x4 slice. The times are simulated.
32 devices in a mesh: pts: 4 (over x, core), snap: 8 (over z, y).
Axes of the slice: x: 2, y: 2, z: 4, core: 2. Of those that a mesh axis runs over, the one named last changes fastest.
Arguments:
- snapshots: float32 [4096, 8192], P('pts', 'snap'), may hold values from -8 to 8
- modes_init: float32 [4096, 128], P('pts'), may hold values from -6 to 6
- coefs_init: float32 [128, 8192], P(None, 'snap'), may hold values from -0.09375 to 0.09375
Outputs:
- modes: float32 [4096, 128], P('pts')
- amplitudes: float32 [128, 8192], P(None, 'snap')
All inputs are finite; a program needn't handle non-finite values.
Results may differ from a plain program's by a relative error of at most 0.0003.
Values sent between devices are 32-bit elements; how exact they have to be, the bound alone decides.
A program may use at most 64 MiB of HBM per device.

v0:
```python
import jax
import jax.numpy as jnp
from jax import lax
from jax.sharding import PartitionSpec as P

OUTER = 2
INNER = 2
HUBER = 1.345
RIDGE = 0.01


def high_dot(left, right):
    return jnp.dot(left, right, preferred_element_type=jnp.float32, precision=lax.Precision.HIGHEST)


def clipped_error(snapshots, modes, coefs, count):
    error = snapshots - high_dot(modes, coefs)
    total = lax.psum(jnp.sum(error * error), ("pts", "snap"))
    limit = HUBER * jnp.sqrt(total / count + 1e-06)
    return jnp.clip(error, -limit, limit)


def shards(snapshots, modes_init, coefs_init):
    modes = modes_init
    coefs = coefs_init
    rows, width = snapshots.shape
    points = rows * lax.axis_size("pts")
    count = float(points * width * lax.axis_size("snap"))
    rank = modes.shape[1]
    eye = jnp.eye(rank, dtype=jnp.float32)
    for outer in range(OUTER):
        gram = lax.psum(high_dot(modes.T, modes), "pts") + RIDGE * eye
        factor = jnp.linalg.cholesky(gram)
        for inner in range(INNER):
            clipped = clipped_error(snapshots, modes, coefs, count)
            product = high_dot(modes.T, clipped)
            share = lax.psum_scatter(product, "pts", scatter_dimension=1, tiled=True)
            span = share.shape[1]
            own = lax.dynamic_slice_in_dim(coefs, lax.axis_index("pts") * span, span, 1)
            own = own + jax.scipy.linalg.cho_solve((factor, True), share)
            coefs = lax.all_gather(own, "pts", axis=1, tiled=True)
        clipped = clipped_error(snapshots, modes, coefs, count)
        hess = lax.psum(high_dot(coefs, coefs.T), "snap") + RIDGE * eye
        hfactor = jnp.linalg.cholesky(hess)
        moment = high_dot(clipped, coefs.T)
        summed = lax.psum(moment, "snap")
        modes = modes + jax.scipy.linalg.cho_solve((hfactor, True), summed.T).T
    return (modes, coefs * jnp.sqrt(jnp.float32(points)))


def solution(mesh):
    in_specs = (P("pts", "snap"), P("pts", None), P(None, "snap"))
    out_specs = (P("pts", None), P(None, "snap"))
    return jax.shard_map(shards, mesh=mesh, in_specs=in_specs, out_specs=out_specs, check_vma=False)
```

profile of v0, /device:TPU:0, one launch (start us, length us, event | category | flops | bytes accessed | tf_op | source)
XLA Modules:
  0.0 692.1 jit_solution(7492501816023668363)
XLA Ops:
  10.1 8.6 %multiply_reduce_fusion.5 = (f32[]{:T(128)}, f32[1024,1024]{1,0:T(8,128)}) fusion(f32[1024,1024]{1,0:T(8,128)} %param.8, f32[1024,128]{1,0:T(8,128)} %param.9, f32[128,1024]{1,0:T(8,128)} %param.10), kind=kOutput, calls=%fused_computation.25 | convolution fusion | flops 1613758464 | bytes 9437188 | tf_op jit(solution)/shard_map/dot_general | solution.py:13
  18.8 42.5 %psum.85 = f32[]{:T(128)} all-reduce(f32[]{:T(128)} %get-tuple-element.11), channel_id=1, replica_groups=mesh['pts'=4,'snap'=8] {'pts','snap'}, use_global_device_ids=true, to_apply=%region_4.6 | all-reduce | flops 1 | bytes 8 | tf_op jit(solution)/shard_map/psum | solution.py:18
  61.9 9.6 %fusion.32 = f32[128,1024]{0,1:T(8,128)} fusion(f32[1024,128]{1,0:T(8,128)S(1)} %copy-done, f32[1024,1024]{1,0:T(8,128)} %get-tuple-element.12, f32[]{:T(128)S(6)} %neg.18, f32[]{:T(128)S(6)} %mul.63), kind=kOutput, calls=%fused_computation.46 | convolution fusion | flops 1612709888 | bytes 5242888 | tf_op jit(solution)/shard_map/dot_general | solution.py:13
  79.4 11.7 %cholesky.74 = f32[128,128]{1,0:T(8,128)S(1)} custom-call(f32[128,128]{1,0:T(8,128)S(1)} %fusion.63), custom_call_target="Cholesky" | custom-call | tf_op jit(solution)/shard_map/jit(cholesky)/cholesky | solution.py:33
  92.4 9.8 %custom-call.16 = f32[1,128,128]{1,2,0:T(8,128)S(1)} custom-call(f32[1,128,128]{2,1,0:T(8,128)S(1)} %fusion.38), custom_call_target="InvertDiagBlocksLowerTriangular" | custom-call | tf_op jit(solution)/shard_map/jit(_cho_solve)/triangular_solve | solution.py:40
  104.7 8.0 %all_gather.12 = f32[128,1024]{1,0:T(8,128)S(1)} all-gather(f32[128,256]{1,0:T(8,128)S(1)} %convolution_add_fusion.3), channel_id=1, replica_groups=mesh['pts'=4,'snap'=8] {'pts'}, dimensions={1}, use_global_device_ids=true | all-gather | bytes 655360 | tf_op jit(solution)/shard_map/all_gather | solution.py:41
  112.6 7.7 %multiply_reduce_fusion.4 = (f32[]{:T(128)}, f32[1024,1024]{0,1:T(8,128)}) fusion(f32[1024,1024]{0,1:T(8,128)} %copy.7, f32[128,1024]{1,0:T(8,128)S(1)} %all_gather.12, f32[1024,128]{1,0:T(8,128)S(1)} %copy-done), kind=kOutput, calls=%fused_computation.21 | convolution fusion | flops 1613758464 | bytes 9437188 | tf_op jit(solution)/shard_map/dot_general | solution.py:13
  120.3 39.7 %psum.86 = f32[]{:T(128)} all-reduce(f32[]{:T(128)} %get-tuple-element.13), channel_id=1, replica_groups=mesh['pts'=4,'snap'=8] {'pts','snap'}, use_global_device_ids=true, to_apply=%region_7.10 | all-reduce | flops 1 | bytes 8 | tf_op jit(solution)/shard_map/psum | solution.py:18
  167.2 22.0 %reduce-scatter.7.cloned.1.call-done = f32[128,256]{0,1:T(8,128)} async-done(((f32[128,1024]{0,1:T(8,128)}), f32[128,256]{0,1:T(8,128)}) %reduce-scatter.7.cloned.1.call-update) | async-done | bytes 131088 | tf_op jit(solution)/shard_map/reduce_scatter | solution.py:37
  197.3 7.6 %multiply_reduce_fusion.3 = (f32[]{:T(128)}, f32[1024,1024]{0,1:T(8,128)}) fusion(f32[1024,1024]{0,1:T(8,128)} %copy.7, f32[128,1024]{1,0:T(8,128)S(1)} %all_gather.13, f32[1024,128]{1,0:T(8,128)S(1)} %copy-done), kind=kOutput, calls=%fused_computation.17 | convolution fusion | flops 1613758464 | bytes 9437188 | tf_op jit(solution)/shard_map/dot_general | solution.py:13
  206.1 40.0 %psum.88 = f32[]{:T(128)} all-reduce(f32[]{:T(128)} %get-tuple-element.15), channel_id=1, replica_groups=mesh['pts'=4,'snap'=8] {'pts','snap'}, use_global_device_ids=true, to_apply=%region_11.14 | all-reduce | flops 1 | bytes 8 | tf_op jit(solution)/shard_map/psum | solution.py:18
  253.0 73.4 %all-reduce.13.cloned.1.call-done = (f32[128,1024]{1,0:T(8,128)}, f32[128,128]{0,1:T(8,128)}) async-done(((f32[128,1024]{1,0:T(8,128)}, f32[128,128]{0,1:T(8,128)}), (f32[128,1024]{1,0:T(8,128)}, f32[128,128]{0,1:T(8,128)})) %all-reduce.13.cloned.1.call-update) | async-done | bytes 589840 | tf_op jit(solution)/shard_map/psum | solution.py:46
  328.2 11.7 %cholesky.85 = f32[128,128]{1,0:T(8,128)S(1)} custom-call(f32[128,128]{1,0:T(8,128)S(1)} %fusion.56), custom_call_target="Cholesky" | custom-call | tf_op jit(solution)/shard_map/jit(cholesky)/cholesky | solution.py:44
  341.3 9.8 %custom-call.18 = f32[1,128,128]{1,2,0:T(8,128)S(1)} custom-call(f32[1,128,128]{2,1,0:T(8,128)S(1)} %fusion.39), custom_call_target="InvertDiagBlocksLowerTriangular" | custom-call | tf_op jit(solution)/shard_map/jit(_cho_solve)/triangular_solve | solution.py:47
  362.2 40.0 %psum.91 = f32[]{:T(128)} all-reduce(f32[]{:T(128)} %get-tuple-element.17), channel_id=1, replica_groups=mesh['pts'=4,'snap'=8] {'pts','snap'}, use_global_device_ids=true, to_apply=%region_15.19 | all-reduce | flops 1 | bytes 8 | tf_op jit(solution)/shard_map/psum | solution.py:18
  410.5 11.7 %cholesky.96 = f32[128,128]{1,0:T(8,128)S(1)} custom-call(f32[128,128]{1,0:T(8,128)S(1)} %fusion.52), custom_call_target="Cholesky" | custom-call | tf_op jit(solution)/shard_map/jit(cholesky)/cholesky | solution.py:33
  423.6 9.8 %custom-call.19 = f32[1,128,128]{1,2,0:T(8,128)S(1)} custom-call(f32[1,128,128]{2,1,0:T(8,128)S(1)} %fusion.40), custom_call_target="InvertDiagBlocksLowerTriangular" | custom-call | tf_op jit(solution)/shard_map/jit(_cho_solve)/triangular_solve | solution.py:40
  434.9 8.1 %all_gather.14 = f32[128,1024]{1,0:T(8,128)S(1)} all-gather(f32[128,256]{1,0:T(8,128)S(1)} %convolution_add_fusion.1), channel_id=1, replica_groups=mesh['pts'=4,'snap'=8] {'pts'}, dimensions={1}, use_global_device_ids=true | all-gather | bytes 655360 | tf_op jit(solution)/shard_map/all_gather | solution.py:41
  450.6 38.7 %psum.92 = f32[]{:T(128)} all-reduce(f32[]{:T(128)} %get-tuple-element.19), channel_id=1, replica_groups=mesh['pts'=4,'snap'=8] {'pts','snap'}, use_global_device_ids=true, to_apply=%region_18.22 | all-reduce | flops 1 | bytes 8 | tf_op jit(solution)/shard_map/psum | solution.py:18
  495.8 22.3 %reduce-scatter.11.cloned.1.call-done = f32[128,256]{1,0:T(8,128)} async-done(((f32[128,1024]{1,0:T(8,128)}), f32[128,256]{1,0:T(8,128)}) %reduce-scatter.11.cloned.1.call-update) | async-done | bytes 131088 | tf_op jit(solution)/shard_map/reduce_scatter | solution.py:37
  535.0 40.2 %psum.94 = f32[]{:T(128)} all-reduce(f32[]{:T(128)} %get-tuple-element.21), channel_id=1, replica_groups=mesh['pts'=4,'snap'=8] {'pts','snap'}, use_global_device_ids=true, to_apply=%region_22.26 | all-reduce | flops 1 | bytes 8 | tf_op jit(solution)/shard_map/psum | solution.py:18
  584.1 73.0 %all-reduce.11.cloned.1.call-done = (f32[128,1024]{1,0:T(8,128)}, f32[128,128]{0,1:T(8,128)}) async-done(((f32[128,1024]{1,0:T(8,128)}, f32[128,128]{0,1:T(8,128)}), (f32[128,1024]{1,0:T(8,128)}, f32[128,128]{0,1:T(8,128)})) %all-reduce.11.cloned.1.call-update) | async-done | bytes 589840 | tf_op jit(solution)/shard_map/psum | solution.py:46
  658.9 11.7 %cholesky.107 = f32[128,128]{1,0:T(8,128)S(1)} custom-call(f32[128,128]{1,0:T(8,128)S(1)} %fusion.45), custom_call_target="Cholesky" | custom-call | tf_op jit(solution)/shard_map/jit(cholesky)/cholesky | solution.py:44
  672.0 9.8 %custom-call.21 = f32[1,128,128]{1,2,0:T(8,128)S(1)} custom-call(f32[1,128,128]{2,1,0:T(8,128)S(1)} %fusion.41), custom_call_target="InvertDiagBlocksLowerTriangular" | custom-call | tf_op jit(solution)/shard_map/jit(_cho_solve)/triangular_solve | solution.py:47
  (76 shorter events, 105.7 us)
Async XLA Ops:
  7.2 70.4 %all-reduce.7.cloned.1.call-start = ((), (), s32[]{:S(2)}) async-start(), calls=%async_computation.4 | async-start | bytes 131072 | tf_op jit(solution)/shard_map/psum | solution.py:32
  10.1 51.9 %copy-start = (f32[1024,128]{1,0:T(8,128)S(1)}, f32[1024,128]{1,0:T(8,128)}, u32[]{:S(2)}) copy-start(f32[1024,128]{1,0:T(8,128)} %param.9) | copy-start | bytes 1572868
  10.1 92.2 %reduce-scatter.5.cloned.1.call-start = ((), (), s32[]{:S(2)}) async-start(), calls=%async_computation.5 | async-start | bytes 655360 | tf_op jit(solution)/shard_map/reduce_scatter | solution.py:37
  71.6 117.6 %reduce-scatter.7.cloned.1.call-start = ((), (), s32[]{:S(2)}) async-start(), calls=%async_computation.6 | async-start | bytes 655360 | tf_op jit(solution)/shard_map/reduce_scatter | solution.py:37
  167.1 159.3 %all-reduce.13.cloned.1.call-start = ((), (), s32[]{:S(2)}) async-start(), calls=%async_computation.11 | async-start | bytes 1179648 | tf_op jit(solution)/shard_map/psum | solution.py:46
  252.5 156.2 %all-reduce.9.cloned.1.call-start = ((), (), s32[]{:S(2)}) async-start(), calls=%async_computation.7 | async-start | bytes 131072 | tf_op jit(solution)/shard_map/psum | solution.py:32
  362.2 71.2 %reduce-scatter.9.cloned.1.call-start = ((), (), s32[]{:S(2)}) async-start(), calls=%async_computation.8 | async-start | bytes 655360 | tf_op jit(solution)/shard_map/reduce_scatter | solution.py:37
  408.6 109.5 %reduce-scatter.11.cloned.1.call-start = ((), (), s32[]{:S(2)}) async-start(), calls=%async_computation.9 | async-start | bytes 655360 | tf_op jit(solution)/shard_map/reduce_scatter | solution.py:37
  495.8 161.4 %all-reduce.11.cloned.1.call-start = ((), (), s32[]{:S(2)}) async-start(), calls=%async_computation.10 | async-start | bytes 1179648 | tf_op jit(solution)/shard_map/psum | solution.py:46
Sparse Core Ops, SparseCore 0:
  10.9 34.2 all-reduce.6
  71.7 21.8 reduce-scatter.4
  167.3 21.8 reduce-scatter.6
  252.7 73.7 all-reduce.12
  362.3 30.6 all-reduce.8
  408.8 21.6 reduce-scatter.8
  495.9 22.2 reduce-scatter.10
  583.4 73.6 all-reduce.10
where the time goes:
time: 698 us; the launch traced here: 692 us
  blocking collectives  270 us (39%)
  waiting for transfers between devices  191 us (27%)
  matrix products  105 us (15%)
  other arithmetic  99.1 us (14%)
  between operations  18.8 us (3%)
    psum x6, blocking collectives, clipped_error(): total = lax.psum(jnp.sum(error * error), ('pts', 'snap'))  241 us
    psum x2, waiting for transfers between devices, shards(): summed = lax.psum(moment, 'snap')  146 us
    dot_general x16, matrix products, high_dot(): jnp.dot(left, right, preferred_element_type=jnp.float32, precision=lax.Pr...  93.5 us
    reduce_scatter x4, waiting for transfers between devices, shards(): share = lax.psum_scatter(product, 'pts', scatter_dimension=1, tiled=True)  44.4 us
    all_gather x4, blocking collectives, shards(): coefs = lax.all_gather(own, 'pts', axis=1, tiled=True)  29.3 us
    another operation x6, other arithmetic, shards(): factor = jnp.linalg.cholesky(gram)  24.8 us
    another operation x6, other arithmetic, shards(): hfactor = jnp.linalg.cholesky(hess)  24.8 us
    another operation x4, other arithmetic, shards(): own = own + jax.scipy.linalg.cho_solve((factor, True), share)  20.9 us
  transfers between devices with their start and end apart: 8, of which 4 were waited for; matrix products, arithmetic and copies ran while one was open for 12% of the time, Pallas kernels for 0%

commit v1 on v0

--- a/solution.py
+++ b/solution.py
@@ -1,3 +1,4 @@
+import functools
 import jax
 import jax.numpy as jnp
 from jax import lax
@@ -7,6 +8,13 @@
 INNER = 2
 HUBER = 1.345
 RIDGE = 0.01
+
+
+def begin_roots(original, mesh_ax):
+    return lax.all_gather(original, axis_name=mesh_ax).sum(axis=0)
+
+
+_wait_spot = functools.partial(begin_roots, mesh_ax="snap")
 
 
 def high_dot(left, right):
@@ -43,7 +51,7 @@
         hess = lax.psum(high_dot(coefs, coefs.T), "snap") + RIDGE * eye
         hfactor = jnp.linalg.cholesky(hess)
         moment = high_dot(clipped, coefs.T)
-        summed = lax.psum(moment, "snap")
+        summed = _wait_spot(moment)
         modes = modes + jax.scipy.linalg.cho_solve((hfactor, True), summed.T).T
     return (modes, coefs * jnp.sqrt(jnp.float32(points)))
 

time: 698 us -> 699 us (level)
    psum x2, waiting for transfers between devices: 146 us -> 40.1 us  [shards(): hess = lax.psum(high_dot(coefs, coefs.T), 'snap') + RIDGE * eye]
    all_gather x0 -> x2, waiting for transfers between devices: none -> 101 us  [begin_roots(): return lax.all_gather(original, axis_name=mesh_ax).sum(axis=0)]
  transfers between devices with their start and end apart: 8 -> 10, of which waited for: 4 -> 6; matrix products, arithmetic and copies ran while one was open for 12% -> 21% of each run, Pallas kernels for 0% -> 0%
where the time goes in v1:
time: 699 us; the launch traced here: 694 us
  blocking collectives  271 us (39%)
  waiting for transfers between devices  186 us (27%)
  matrix products  106 us (15%)
  other arithmetic  104 us (15%)
  between operations  19.1 us (3%)
    psum x6, blocking collectives, clipped_error(): total = lax.psum(jnp.sum(error * error), ('pts', 'snap'))  242 us
    all_gather x2, waiting for transfers between devices, begin_roots(): return lax.all_gather(original, axis_name=mesh_ax).sum(axis=0)  101 us
    dot_general x16, matrix products, high_dot(): jnp.dot(left, right, preferred_element_type=jnp.float32, precision=lax.Pr...  96.6 us
    reduce_scatter x4, waiting for transfers between devices, shards(): share = lax.psum_scatter(product, 'pts', scatter_dimension=1, tiled=True)  44 us
    psum x2, waiting for transfers between devices, shards(): hess = lax.psum(high_dot(coefs, coefs.T), 'snap') + RIDGE * eye  40.1 us
    all_gather x4, blocking collectives, shards(): coefs = lax.all_gather(own, 'pts', axis=1, tiled=True)  29.3 us
    another operation x6, other arithmetic, shards(): hfactor = jnp.linalg.cholesky(hess)  24.8 us
    another operation x6, other arithmetic, shards(): factor = jnp.linalg.cholesky(gram)  24.8 us
  transfers between devices with their start and end apart: 10, of which 6 were waited for; matrix products, arithmetic and copies ran while one was open for 21% of the time, Pallas kernels for 0%

profile of v1, /device:TPU:0, one launch (start us, length us, event | category | flops | bytes accessed | tf_op | source)
XLA Modules:
  0.0 693.6 jit_solution(12822842193598607610)
XLA Ops:
  10.1 8.6 %multiply_reduce_fusion.5 = (f32[]{:T(128)}, f32[1024,1024]{1,0:T(8,128)}) fusion(f32[1024,1024]{1,0:T(8,128)} %param.8, f32[1024,128]{1,0:T(8,128)} %param.9, f32[128,1024]{1,0:T(8,128)} %param.10), kind=kOutput, calls=%fused_computation.25 | convolution fusion | flops 1613758464 | bytes 9437188 | tf_op jit(solution)/shard_map/dot_general | solution.py:21
  18.8 42.7 %psum.71 = f32[]{:T(128)} all-reduce(f32[]{:T(128)} %get-tuple-element.7), channel_id=1, replica_groups=mesh['pts'=4,'snap'=8] {'pts','snap'}, use_global_device_ids=true, to_apply=%region_4.6 | all-reduce | flops 1 | bytes 8 | tf_op jit(solution)/shard_map/psum | solution.py:26
  62.2 9.6 %fusion.32 = f32[128,1024]{0,1:T(8,128)} fusion(f32[1024,128]{1,0:T(8,128)S(1)} %copy-done, f32[1024,1024]{1,0:T(8,128)} %get-tuple-element.8, f32[]{:T(128)S(6)} %neg.18, f32[]{:T(128)S(6)} %mul.63), kind=kOutput, calls=%fused_computation.46 | convolution fusion | flops 1612709888 | bytes 5242888 | tf_op jit(solution)/shard_map/dot_general | solution.py:21
  79.2 11.7 %cholesky.74 = f32[128,128]{1,0:T(8,128)S(1)} custom-call(f32[128,128]{1,0:T(8,128)S(1)} %fusion.65), custom_call_target="Cholesky" | custom-call | tf_op jit(solution)/shard_map/jit(cholesky)/cholesky | solution.py:41
  92.3 9.8 %custom-call.16 = f32[1,128,128]{1,2,0:T(8,128)S(1)} custom-call(f32[1,128,128]{2,1,0:T(8,128)S(1)} %fusion.42), custom_call_target="InvertDiagBlocksLowerTriangular" | custom-call | tf_op jit(solution)/shard_map/jit(_cho_solve)/triangular_solve | solution.py:48
  120.2 39.8 %psum.72 = f32[]{:T(128)} all-reduce(f32[]{:T(128)} %get-tuple-element.9), channel_id=1, replica_groups=mesh['pts'=4,'snap'=8] {'pts','snap'}, use_global_device_ids=true, to_apply=%region_7.10 | all-reduce | flops 1 | bytes 8 | tf_op jit(solution)/shard_map/psum | solution.py:26
  167.1 22.0 %reduce-scatter.7.cloned.1.call-done = f32[128,256]{0,1:T(8,128)} async-done(((f32[128,1024]{0,1:T(8,128)}), f32[128,256]{0,1:T(8,128)}) %reduce-scatter.7.cloned.1.call-update) | async-done | bytes 131088 | tf_op jit(solution)/shard_map/reduce_scatter | solution.py:45
  206.1 40.4 %psum.74 = f32[]{:T(128)} all-reduce(f32[]{:T(128)} %get-tuple-element.11), channel_id=1, replica_groups=mesh['pts'=4,'snap'=8] {'pts','snap'}, use_global_device_ids=true, to_apply=%region_11.14 | all-reduce | flops 1 | bytes 8 | tf_op jit(solution)/shard_map/psum | solution.py:26
  247.2 9.6 %fusion.9 = f32[1024,128]{1,0:T(8,128)} fusion(f32[128,1024]{1,0:T(8,128)S(1)} %all_gather.25, f32[1024,1024]{0,1:T(8,128)} %get-tuple-element.12, f32[]{:T(128)S(6)} %neg.20, f32[]{:T(128)S(6)} %mul.67), kind=kOutput, calls=%fused_computation.14 | convolution fusion | flops 1612709888 | bytes 5242888 | tf_op jit(solution)/shard_map/dot_general | solution.py:21
  257.6 18.5 %all-reduce.7.cloned.1.call-done = f32[128,128]{0,1:T(8,128)} async-done(((f32[128,128]{0,1:T(8,128)}), f32[128,128]{0,1:T(8,128)}) %all-reduce.7.cloned.1.call-update) | async-done | bytes 65552 | tf_op jit(solution)/shard_map/psum | solution.py:51
  277.9 11.7 %cholesky.85 = f32[128,128]{1,0:T(8,128)S(1)} custom-call(f32[128,128]{1,0:T(8,128)S(1)} %fusion.58), custom_call_target="Cholesky" | custom-call | tf_op jit(solution)/shard_map/jit(cholesky)/cholesky | solution.py:52
  290.9 9.8 %custom-call.18 = f32[1,128,128]{1,2,0:T(8,128)S(1)} custom-call(f32[1,128,128]{2,1,0:T(8,128)S(1)} %fusion.43), custom_call_target="InvertDiagBlocksLowerTriangular" | custom-call | tf_op jit(solution)/shard_map/jit(_cho_solve)/triangular_solve | solution.py:55
  300.7 50.7 %all-gather.5.cloned.1.call-done = f32[8192,128]{1,0:T(8,128)} async-done(((f32[1024,128]{1,0:T(8,128)}), f32[8192,128]{1,0:T(8,128)}) %all-gather.5.cloned.1.call-update) | async-done | bytes 4194320 | tf_op jit(solution)/shard_map/all_gather | solution.py:14
  364.0 39.3 %psum.76 = f32[]{:T(128)} all-reduce(f32[]{:T(128)} %get-tuple-element.13), channel_id=1, replica_groups=mesh['pts'=4,'snap'=8] {'pts','snap'}, use_global_device_ids=true, to_apply=%region_15.19 | all-reduce | flops 1 | bytes 8 | tf_op jit(solution)/shard_map/psum | solution.py:26
  411.6 11.7 %cholesky.96 = f32[128,128]{1,0:T(8,128)S(1)} custom-call(f32[128,128]{1,0:T(8,128)S(1)} %fusion.55), custom_call_target="Cholesky" | custom-call | tf_op jit(solution)/shard_map/jit(cholesky)/cholesky | solution.py:41
  424.7 9.8 %custom-call.19 = f32[1,128,128]{1,2,0:T(8,128)S(1)} custom-call(f32[1,128,128]{2,1,0:T(8,128)S(1)} %fusion.44), custom_call_target="InvertDiagBlocksLowerTriangular" | custom-call | tf_op jit(solution)/shard_map/jit(_cho_solve)/triangular_solve | solution.py:48
  436.0 8.2 %all_gather.28 = f32[128,1024]{1,0:T(8,128)S(1)} all-gather(f32[128,256]{1,0:T(8,128)S(1)} %convolution_add_fusion.1), channel_id=1, replica_groups=mesh['pts'=4,'snap'=8] {'pts'}, dimensions={1}, use_global_device_ids=true | all-gather | bytes 655360 | tf_op jit(solution)/shard_map/all_gather | solution.py:49
  451.7 39.1 %psum.77 = f32[]{:T(128)} all-reduce(f32[]{:T(128)} %get-tuple-element.15), channel_id=1, replica_groups=mesh['pts'=4,'snap'=8] {'pts','snap'}, use_global_device_ids=true, to_apply=%region_18.22 | all-reduce | flops 1 | bytes 8 | tf_op jit(solution)/shard_map/psum | solution.py:26
  497.3 22.0 %reduce-scatter.11.cloned.1.call-done = f32[128,256]{1,0:T(8,128)} async-done(((f32[128,1024]{1,0:T(8,128)}), f32[128,256]{1,0:T(8,128)}) %reduce-scatter.11.cloned.1.call-update) | async-done | bytes 131088 | tf_op jit(solution)/shard_map/reduce_scatter | solution.py:45
  536.3 40.4 %psum.79 = f32[]{:T(128)} all-reduce(f32[]{:T(128)} %get-tuple-element.17), channel_id=1, replica_groups=mesh['pts'=4,'snap'=8] {'pts','snap'}, use_global_device_ids=true, to_apply=%region_22.26 | all-reduce | flops 1 | bytes 8 | tf_op jit(solution)/shard_map/psum | solution.py:26
  584.6 21.7 %all-reduce.11.cloned.1.call-done = f32[128,128]{0,1:T(8,128)} async-done(((f32[128,128]{0,1:T(8,128)}), f32[128,128]{0,1:T(8,128)}) %all-reduce.11.cloned.1.call-update) | async-done | bytes 65552 | tf_op jit(solution)/shard_map/psum | solution.py:51
  608.0 11.7 %cholesky.107 = f32[128,128]{1,0:T(8,128)S(1)} custom-call(f32[128,128]{1,0:T(8,128)S(1)} %fusion.48), custom_call_target="Cholesky" | custom-call | tf_op jit(solution)/shard_map/jit(cholesky)/cholesky | solution.py:52
  621.1 9.8 %custom-call.21 = f32[1,128,128]{1,2,0:T(8,128)S(1)} custom-call(f32[1,128,128]{2,1,0:T(8,128)S(1)} %fusion.45), custom_call_target="InvertDiagBlocksLowerTriangular" | custom-call | tf_op jit(solution)/shard_map/jit(_cho_solve)/triangular_solve | solution.py:55
  630.9 50.7 %all-gather.7.cloned.1.call-done = f32[8192,128]{1,0:T(8,128)} async-done(((f32[1024,128]{1,0:T(8,128)}), f32[8192,128]{1,0:T(8,128)}) %all-gather.7.cloned.1.call-update) | async-done | bytes 4194320 | tf_op jit(solution)/shard_map/all_gather | solution.py:14
  (84 shorter events, 125.2 us)
Async XLA Ops:
  7.2 70.2 %all-reduce.5.cloned.1.call-start = ((), (), s32[]{:S(2)}) async-start(), calls=%async_computation.4 | async-start | bytes 131072 | tf_op jit(solution)/shard_map/psum | solution.py:40
  10.1 52.1 %copy-start = (f32[1024,128]{1,0:T(8,128)S(1)}, f32[1024,128]{1,0:T(8,128)}, u32[]{:S(2)}) copy-start(f32[1024,128]{1,0:T(8,128)} %param.9) | copy-start | bytes 1572868
  10.1 92.0 %reduce-scatter.5.cloned.1.call-start = ((), (), s32[]{:S(2)}) async-start(), calls=%async_computation.5 | async-start | bytes 655360 | tf_op jit(solution)/shard_map/reduce_scatter | solution.py:45
  71.8 117.3 %reduce-scatter.7.cloned.1.call-start = ((), (), s32[]{:S(2)}) async-start(), calls=%async_computation.6 | async-start | bytes 655360 | tf_op jit(solution)/shard_map/reduce_scatter | solution.py:45
  167.1 109.0 %all-reduce.7.cloned.1.call-start = ((), (), s32[]{:S(2)}) async-start(), calls=%async_computation.7 | async-start | bytes 131072 | tf_op jit(solution)/shard_map/psum | solution.py:51
  206.1 145.4 %all-gather.5.cloned.1.call-start = ((), (), s32[]{:S(2)}) async-start(), calls=%async_computation.12 | async-start | bytes 4718592 | tf_op jit(solution)/shard_map/all_gather | solution.py:14
  256.8 152.9 %all-reduce.9.cloned.1.call-start = ((), (), s32[]{:S(2)}) async-start(), calls=%async_computation.8 | async-start | bytes 131072 | tf_op jit(solution)/shard_map/psum | solution.py:40
  363.9 70.5 %reduce-scatter.9.cloned.1.call-start = ((), (), s32[]{:S(2)}) async-start(), calls=%async_computation.9 | async-start | bytes 655360 | tf_op jit(solution)/shard_map/reduce_scatter | solution.py:45
  409.7 109.6 %reduce-scatter.11.cloned.1.call-start = ((), (), s32[]{:S(2)}) async-start(), calls=%async_computation.10 | async-start | bytes 655360 | tf_op jit(solution)/shard_map/reduce_scatter | solution.py:45
  497.3 109.0 %all-reduce.11.cloned.1.call-start = ((), (), s32[]{:S(2)}) async-start(), calls=%async_computation.11 | async-start | bytes 131072 | tf_op jit(solution)/shard_map/psum | solution.py:51
  536.2 145.4 %all-gather.7.cloned.1.call-start = ((), (), s32[]{:S(2)}) async-start(), calls=%async_computation.13 | async-start | bytes 4718592 | tf_op jit(solution)/shard_map/all_gather | solution.py:14
Sparse Core Ops, SparseCore 0:
  10.9 34.2 all-reduce.4
  71.9 21.7 reduce-scatter.4
  167.2 21.8 reduce-scatter.6
  206.2 69.8 all-reduce.6
  278.6 72.8 all-gather.4
  364.1 30.0 all-reduce.8
  409.8 22.5 reduce-scatter.8
  497.4 21.8 reduce-scatter.10
  536.3 69.8 all-reduce.10
  608.8 72.8 all-gather.6
